TPU v7x, 32 devices: a whole 2x2x4 slice. The times are simulated.
32 devices in a mesh: zone: 4 (over y, x), slab: 8 (over z, core).
Axes of the slice: x: 2, y: 2, z: 4, core: 2. Of those that a mesh axis runs over, the one named last changes fastest.
Arguments:
- tracers: float32 [4, 4, 2048, 2048], P('zone', None, 'slab'), may hold values from -6 to 6
- velocity: float32 [4, 2, 2048, 2048], P('zone', None, 'slab'), may hold values from -0.2 to 0.2
- diffusivity: float32 [4], replicated, may hold values from 0.02 to 0.12
- owner_dev: int32 [512, 2], P('slab'), may hold values from 0 to 23, all different within a row; in each aligned block of 64 rows (0 to 63, 64 to 127, ...) at most 7 rows name the same one
- owner_seg: int32 [512, 2], P('slab'), may hold values from 0 to 63
- intersection: float32 [512, 2], P('slab'), may hold values from 0.2 to 1
Outputs:
- updated: float32 [4, 4, 2048, 2048], P('zone', None, 'slab')
Inputs may be any that keep to these rules, and one draw needn't show every extreme that they name: owner_dev names workpiece slab zone * 8 + slab; the 2 entries of a row differ; the rows of one pin slab name one workpiece slab at most 7 times, and some name one exactly 7 times.
All inputs are finite; a program needn't handle non-finite values.
Results may differ from a plain program's by a relative error of at most 0.00007.
Values sent between devices are 32-bit elements; how exact they have to be, the bound alone decides.
No kernel may reach another device: no remote copies, remote signals or barrier semaphores. Data moves between devices by JAX's collectives and lax.ppermute only.
A program may use at most 128 MiB of HBM per device.

v0:
```python
import jax
import jax.numpy as jnp
from jax import lax
from jax.sharding import PartitionSpec as P

SEG = 32
COUPLE = 0.5


def extended(block, sides, width):
    for axis, dim in sides:
        count = lax.axis_size(axis)
        forward = [(i, i + 1) for i in range(count - 1)]
        backward = [(target, source) for source, target in forward]
        low = lax.ppermute(
            lax.slice_in_dim(block, block.shape[dim] - width, None, axis=dim), axis, forward
        )
        high = lax.ppermute(lax.slice_in_dim(block, 0, width, axis=dim), axis, backward)
        block = jnp.concatenate([low, block, high], axis=dim)
    return block


def from_root(block, axis, owner):
    block = jnp.where(lax.axis_index(axis) == owner, block, jnp.zeros_like(block))
    return lax.psum(block, axis)


def advance(center, upper_row, lower_row, velocity, diffusivity):
    left_cells = jnp.roll(center, 1, axis=3)
    right_cells = jnp.roll(center, -1, axis=3)
    along_rows = velocity[:, 0][:, None]
    along_cols = velocity[:, 1][:, None]
    transport = jnp.maximum(along_rows, 0.0) * (center - upper_row) + jnp.minimum(
        along_rows, 0.0
    ) * (lower_row - center)
    transport = (
        transport
        + jnp.maximum(along_cols, 0.0) * (center - left_cells)
        + jnp.minimum(along_cols, 0.0) * (right_cells - center)
    )
    laplace = upper_row + lower_row + left_cells + right_cells - 4.0 * center
    return center + diffusivity[None, :, None, None] * laplace - transport


def shards(tracers, velocity, diffusivity, owner_dev, owner_seg, intersection):
    zone_count = lax.axis_size("zone")
    slab_count = lax.axis_size("slab")
    zone_index = lax.axis_index("zone")
    padded = extended(tracers, (("slab", 2),), 1)
    stepped = advance(
        padded[:, :, 1:-1], padded[:, :, :-2], padded[:, :, 2:], velocity, diffusivity
    )
    tracer_count = tracers.shape[1]
    row_count = tracers.shape[2]
    col_count = tracers.shape[3]
    seg_count = col_count // SEG
    payload = tracer_count * SEG
    own_face = (
        tracers[0, :, row_count - 1, :]
        .reshape(tracer_count, seg_count, SEG)
        .transpose(1, 0, 2)
        .reshape(seg_count, payload)
    )
    pin_face = from_root(own_face, "zone", zone_count - 1)
    fanout = owner_dev.shape[1]
    item_count = owner_dev.shape[0] * fanout
    target_dev = owner_dev.reshape(item_count)
    target_seg = owner_seg.reshape(item_count)
    weight = intersection.reshape(item_count)
    in_zone = target_dev // slab_count == zone_index
    target_slab = target_dev % slab_count
    pin_values = jnp.repeat(pin_face, fanout, axis=0)
    highest = lax.Precision.HIGHEST
    zone_faces = lax.all_gather(own_face, "slab", axis=0, tiled=True)
    slot_ids = jnp.arange(slab_count * seg_count, dtype=jnp.int32)
    picker = (
        ((target_slab * seg_count + target_seg)[:, None] == slot_ids[None, :]) & in_zone[:, None]
    ).astype(jnp.float32)
    owner_values = jnp.dot(picker, zone_faces, precision=highest)
    item_flux = jnp.where(in_zone, weight, 0.0)[:, None] * (pin_values - owner_values)
    inflow = lax.psum_scatter(
        jnp.dot(picker.T, item_flux, precision=highest), "slab", scatter_dimension=0, tiled=True
    )
    pin_part = jnp.sum(item_flux.reshape(seg_count, fanout, payload), axis=1)
    pin_total = lax.psum(pin_part, "zone")
    is_pin = zone_index == zone_count - 1
    coupling = COUPLE * inflow - jnp.where(is_pin, COUPLE * pin_total, 0.0)
    coupling = (
        coupling.reshape(seg_count, tracer_count, SEG)
        .transpose(1, 0, 2)
        .reshape(tracer_count, col_count)
    )
    return stepped.at[0, :, row_count - 1, :].add(coupling)


def solution(mesh):
    placed = (
        P("zone", None, "slab", None),
        P("zone", None, "slab", None),
        P(),
        P("slab", None),
        P("slab", None),
        P("slab", None),
    )
    return jax.shard_map(
        shards, mesh=mesh, in_specs=placed, out_specs=P("zone", None, "slab", None), check_vma=False
    )
```

profile of v0, /device:TPU:8, one launch (start us, length us, event | category | flops | bytes accessed | tf_op | source)
XLA Modules:
  0.0 117.2 jit_solution(10784930607515676139)
XLA Ops:
  6.5 1.2 slice_reduce_fusion
  7.9 14.4 %all_gather.3 = f32[512,128]{1,0:T(8,128)S(1)} all-gather(f32[64,128]{1,0:T(8,128)S(1)} %copy.61), channel_id=1, replica_groups=mesh['zone'=4,'slab'=8] {'slab'}, dimensions={0}, use_global_device_ids=true | all-gather | bytes 294912 | tf_op jit(solution)/shard_map/all_gather | solution.py:74
  22.4 16.3 %psum.14 = f32[64,128]{1,0:T(8,128)S(1)} all-reduce(f32[64,128]{1,0:T(8,128)S(1)} %broadcast_select_fusion.1), channel_id=1, replica_groups=mesh['zone'=4,'slab'=8] {'zone'}, use_global_device_ids=true, to_apply=%region_1.2 | all-reduce | flops 8192 | bytes 65536 | tf_op jit(solution)/shard_map/psum | solution.py:25
  38.7 0.8 copy.57
  39.5 0.1 reshape.148
  39.6 0.8 copy.59
  40.4 0.1 reshape.150
  40.5 0.8 copy.58
  41.3 0.1 reshape.149
  41.5 0.3 fusion.14
  41.8 1.2 fusion.16
  43.0 1.9 %collective-permute-start = (f32[1,4,1,2048]{3,2,1,0:T(1,128)S(1)}, f32[1,4,1,2048]{3,2,1,0:T(1,128)S(1)}, u32[]{:S(2)}, u32[]{:S(2)}) collective-permute-start(f32[1,4,1,2048]{3,2,1,0:T(1,128)S(1)} %get-tuple-element.21), channel_id=1, source_target_pairs={{0,1},{1,2},{2,3},{3,4},{4,5},{5,6},{6,7},{8,9},{9,10},{10,11},{11... | collective-permute-start | bytes 98312 | tf_op jit(solution)/shard_map/ppermute | solution.py:15
  44.9 3.9 %collective-permute-start.1 = (f32[1,4,1,2048]{3,2,1,0:T(1,128)S(1)}, f32[1,4,1,2048]{3,2,1,0:T(1,128)S(1)}, u32[]{:S(2)}, u32[]{:S(2)}) collective-permute-start(f32[1,4,1,2048]{3,2,1,0:T(1,128)S(1)} %get-tuple-element.20), channel_id=1, source_target_pairs={{1,0},{2,1},{3,2},{4,3},{5,4},{6,5},{7,6},{9,8},{10,9},{11,10},{12... | collective-permute-start | bytes 98312 | tf_op jit(solution)/shard_map/ppermute | solution.py:18
  48.9 13.3 %fusion.28 = (f32[1,4,256,2047]{3,2,1,0:T(8,128)}, f32[1,4,256,2047]{3,2,1,0:T(8,128)}) fusion(f32[1,4,256,2048]{3,2,1,0:T(8,128)} %param.8), kind=kLoop, calls=%fused_computation.47 | loop fusion | bytes 33538048 | tf_op jit(solution)/shard_map/jit(_roll_static)/slice | solution.py:29
  62.1 1.4 %fusion.27 = (f32[1,4,256,1]{3,2,1,0:T(8,128)S(1)}, f32[1,4,256,1]{3,2,1,0:T(8,128)S(1)}) fusion(f32[1,4,256,2048]{3,2,1,0:T(8,128)} %param.8), kind=kLoop, calls=%fused_computation.46 | loop fusion | bytes 16384 | tf_op jit(solution)/shard_map/jit(_roll_static)/slice | solution.py:29
  63.6 2.9 %maximum_bitcast_fusion.1 = (f32[256,2048]{1,0:T(8,128)S(1)}, f32[256,2048]{1,0:T(8,128)}, f32[256,2048]{1,0:T(8,128)}, f32[256,2048]{1,0:T(8,128)}) fusion(f32[1,2,256,2048]{3,2,1,0:T(8,128)S(1)} %copy-done), kind=kLoop, calls=%fused_computation.21 | loop fusion | flops 2097152 | bytes 12582912 | tf_op jit(solution)/shard_map/mul | solution.py:33
  66.5 0.6 fusion.29
  67.1 2.0 %and_reduce_fusion = pred[]{:T(512)} fusion(s32[4]{0:T(128)S(1)} %copy-done.2, s32[1]{0:T(128)} %constant.60.clone.1, s32[1]{0:T(128)} %get-tuple-element.31, s32[1]{0:T(128)} %get-tuple-element.30), kind=kLoop, calls=%fused_computation.36 | loop fusion | flops 27 | bytes 29 | tf_op jit(solution)/shard_map/reduce.1
  69.2 14.3 %psum.15 = f32[64,128]{1,0:T(8,128)S(1)} all-reduce(f32[64,128]{1,0:T(8,128)S(1)} %reduce_sum.9), channel_id=1, replica_groups=mesh['zone'=4,'slab'=8] {'zone'}, use_global_device_ids=true, to_apply=%region_4.5 | all-reduce | flops 8192 | bytes 65536 | tf_op jit(solution)/shard_map/psum | solution.py:85
  83.5 21.2 %fusion.6 = f32[1,4,256,2048]{3,2,1,0:T(8,128)} fusion(f32[1,4,256,2048]{3,2,1,0:T(8,128)} %param.8, f32[1,4,1,2048]{3,2,1,0:T(1,128)S(1)} %collective-permute-done.1, f32[1,4,1,2048]{3,2,1,0:T(1,128)S(1)} %collective-permute-done, f32[1,4,256,1]{3,2,1,0:T(8,128)S(1)} %get-tuple-element.23, f32[1,4,256,2047]{3,2,1,0:T(8,128)} %get-tuple-element.25, ...), kind=kLoop, calls=%fused_computation.7 | loop fusion | flops 48234496 | bytes 42008592 | tf_op jit(solution)/shard_map/sub | solution.py:42
  104.7 0.8 select_subtract_fusion
  105.7 0.1 reshape.156
  105.8 2.2 %broadcast_select_fusion = f32[1,4,1,2048]{3,2,1,0:T(1,128)S(1)} fusion(pred[]{:T(512)} %and_reduce_fusion, f32[1,4,1,2048]{3,2,1,0:T(1,128)S(1)} %reshape.156, f32[1,4,256,2048]{3,2,1,0:T(8,128)} %fusion.6, s32[]{:T(128)} %bitcast.4), kind=kLoop, calls=%fused_computation.31 | loop fusion | flops 16384 | bytes 98309 | tf_op jit(solution)/shard_map/select.1
  108.0 2.4 %scatter-add.4 = f32[1,4,256,2048]{3,2,1,0:T(8,128)} dynamic-update-slice(f32[1,4,256,2048]{3,2,1,0:T(8,128)} %fusion.6, f32[1,4,1,2048]{3,2,1,0:T(1,128)S(1)} %broadcast_select_fusion, s32[]{:T(128)} %constant.58.clone.1, s32[]{:T(128)} %constant.58.clone.1, s32[]{:T(128)} %bitcast.4, s32[]{:T(128)} %constant.58.clone.1) | dynamic-update-slice | bytes 65540 | tf_op jit(solution)/shard_map/scatter-add | solution.py:93
  (22 shorter events, 0.6 us)
Async XLA Ops:
  6.5 98.2 %reduce-scatter.2.cloned.1.call-start = ((), (), s32[]{:S(2)}) async-start(), calls=%async_computation.1 | async-start | bytes 294912 | tf_op jit(solution)/shard_map/reduce_scatter | solution.py:81
  43.0 40.5 %collective-permute-start = (f32[1,4,1,2048]{3,2,1,0:T(1,128)S(1)}, f32[1,4,1,2048]{3,2,1,0:T(1,128)S(1)}, u32[]{:S(2)}, u32[]{:S(2)}) collective-permute-start(f32[1,4,1,2048]{3,2,1,0:T(1,128)S(1)} %get-tuple-element.21), channel_id=1, source_target_pairs={{0,1},{1,2},{2,3},{3,4},{4,5},{5,6},{6,7},{8,9},{9,10},{10,11},{11... | collective-permute-start | bytes 98312 | tf_op jit(solution)/shard_map/ppermute | solution.py:15
  44.9 18.7 %copy-start = (f32[1,2,256,2048]{3,2,1,0:T(8,128)S(1)}, f32[1,2,256,2048]{3,2,1,0:T(8,128)}, u32[]{:S(2)}) copy-start(f32[1,2,256,2048]{3,2,1,0:T(8,128)} %param.9) | copy-start | bytes 12582916
  44.9 38.5 %collective-permute-start.1 = (f32[1,4,1,2048]{3,2,1,0:T(1,128)S(1)}, f32[1,4,1,2048]{3,2,1,0:T(1,128)S(1)}, u32[]{:S(2)}, u32[]{:S(2)}) collective-permute-start(f32[1,4,1,2048]{3,2,1,0:T(1,128)S(1)} %get-tuple-element.20), channel_id=1, source_target_pairs={{1,0},{2,1},{3,2},{4,3},{5,4},{6,5},{7,6},{9,8},{10,9},{11,10},{12... | collective-permute-start | bytes 98312 | tf_op jit(solution)/shard_map/ppermute | solution.py:18
  62.1 5.0 %copy-start.2 = (s32[4]{0:T(128)S(1)}, s32[4]{0:T(128)}, u32[]{:S(2)}) copy-start(s32[4]{0:T(128)} %constant.61.clone.1) | copy-start | bytes 52
  62.1 21.4 %copy-start.1 = (f32[4]{0:T(128)S(1)}, f32[4]{0:T(128)}, u32[]{:S(2)}) copy-start(f32[4]{0:T(128)} %param.10) | copy-start | bytes 52
Sparse Core Ops, SparseCore 0:
  43.1 26.0 reduce-scatter.1
where the time goes:
time: 118 us; the launch traced here: 117 us
  blocking collectives  45 us (38%)
  other arithmetic  29.1 us (25%)
  local copies, waits for them, and re-layouts  22.2 us (19%)
  between operations  13.5 us (11%)
  starting transfers between devices  5.83 us (5%)
  matrix products  1.48 us (1%)
    sub x1, other arithmetic, advance(): return center + diffusivity[None, :, None, None] * laplace - transport  21.2 us
    psum x1, blocking collectives, from_root(): return lax.psum(block, axis)  16.3 us
    slice x2, local copies, waits for them, and re-layouts, advance(): left_cells = jnp.roll(center, 1, axis=3)  14.7 us
    all_gather x1, blocking collectives, shards(): zone_faces = lax.all_gather(own_face, 'slab', axis=0, tiled=True)  14.4 us
    psum x1, blocking collectives, shards(): pin_total = lax.psum(pin_part, 'zone')  14.3 us
    another operation x3, other arithmetic  4.18 us
    ppermute x1, starting transfers between devices, extended(): lax.ppermute(lax.slice_in_dim(block, 0, width, axis=dim), axis, backward)  3.91 us
    mul x1, other arithmetic, advance(): jnp.maximum(along_rows, 0.0) * (center - upper_row)  2.91 us
  transfers between devices with their start and end apart: 3, of which 0 were waited for; matrix products, arithmetic and copies ran while one was open for 35% of the time, Pallas kernels for 0%

commit v1 on v0

--- a/solution.py
+++ b/solution.py
@@ -71,7 +71,24 @@
     target_slab = target_dev % slab_count
     pin_values = jnp.repeat(pin_face, fanout, axis=0)
     highest = lax.Precision.HIGHEST
-    zone_faces = lax.all_gather(own_face, "slab", axis=0, tiled=True)
+
+    def make_works(piece_in):
+        size_here = lax.axis_size("slab")
+        bank = [(dd, (dd + 1) % size_here) for dd in range(size_here)]
+        seen = [(dd, (dd - 1) % size_here) for dd in range(size_here)]
+        tile_out, carry_out = ([piece_in], [piece_in])
+        for _ in range(size_here // 2):
+            tile_out.append(lax.ppermute(tile_out[-1], "slab", bank))
+        dev_i = 0
+        while dev_i < (size_here - 1) // 2:
+            carry_out.append(lax.ppermute(carry_out[-1], "slab", perm=seen))
+            dev_i = dev_i + 1
+        parts_out = jnp.concatenate([*tile_out[::-1], *carry_out[1:]], axis=0)
+        return jnp.roll(
+            parts_out, (lax.axis_index("slab") - size_here // 2) * piece_in.shape[0], axis=0
+        )
+
+    zone_faces = make_works(own_face)
     slot_ids = jnp.arange(slab_count * seg_count, dtype=jnp.int32)
     picker = (
         ((target_slab * seg_count + target_seg)[:, None] == slot_ids[None, :]) & in_zone[:, None]

time: 118 us -> 124 us (1.051)
  the two profiles are of different devices: /device:TPU:8 before, /device:TPU:0 now
where the time goes in v1:
time: 124 us; the launch traced here: 123 us
  other arithmetic  32.9 us (27%)
  blocking collectives  32.1 us (26%)
  local copies, waits for them, and re-layouts  23.5 us (19%)
  starting transfers between devices  15.1 us (12%)
  between operations  13.6 us (11%)
  waiting for transfers between devices  3.33 us (3%)
  matrix products  2.54 us (2%)
    sub x1, other arithmetic, advance(): return center + diffusivity[None, :, None, None] * laplace - transport  21.4 us
    psum x1, blocking collectives, from_root(): return lax.psum(block, axis)  17.9 us
    slice x2, local copies, waits for them, and re-layouts, advance(): left_cells = jnp.roll(center, 1, axis=3)  14.7 us
    psum x1, blocking collectives, shards(): pin_total = lax.psum(pin_part, 'zone')  14.2 us
    ppermute x3, starting transfers between devices, make_works(): carry_out.append(lax.ppermute(carry_out[-1], 'slab', perm=seen))  10.2 us
    mul x1, other arithmetic, advance(): jnp.maximum(along_rows, 0.0) * (center - upper_row)  5.35 us
    another operation x3, other arithmetic  4.73 us
    ppermute x4, waiting for transfers between devices, make_works(): tile_out.append(lax.ppermute(tile_out[-1], 'slab', bank))  3.28 us
  transfers between devices with their start and end apart: 10, of which 2 were waited for; matrix products, arithmetic and copies ran while one was open for 42% of the time, Pallas kernels for 0%

profile of v1, /device:TPU:0, one launch (start us, length us, event | category | flops | bytes accessed | tf_op | source)
XLA Modules:
  0.0 123.0 jit_solution(18359484680694840704)
XLA Ops:
  6.5 1.7 %slice_reduce_fusion = (f32[4,2048]{1,0:T(4,128)S(1)}, f32[1,4,1,2048]{3,2,1,0:T(1,128)}, f32[1,4,1,2048]{3,2,1,0:T(1,128)}) fusion(f32[1,4,256,2048]{3,2,1,0:T(8,128)} %param.8), kind=kLoop, calls=%fused_computation.47 | loop fusion | bytes 163840 | tf_op jit(solution)/shard_map/slice | solution.py:16
  9.0 4.1 %collective-permute-start.6 = (f32[64,128]{0,1:T(8,128)S(1)}, f32[64,128]{0,1:T(8,128)S(1)}, u32[]{:S(2)}, u32[]{:S(2)}) collective-permute-start(f32[64,128]{0,1:T(8,128)S(1)} %bitcast.18), channel_id=1, source_target_pairs={{0,7},{1,0},{2,1},{3,2},{4,3},{5,4},{6,5},{7,6},{8,15},{9,8},{10,9... | collective-permute-start | bytes 98312 | tf_op jit(solution)/shard_map/ppermute | solution.py:84
  13.1 1.9 %collective-permute-start = (f32[1,4,1,2048]{3,2,1,0:T(1,128)}, f32[1,4,1,2048]{3,2,1,0:T(1,128)}, u32[]{:S(2)}, u32[]{:S(2)}) collective-permute-start(f32[1,4,1,2048]{3,2,1,0:T(1,128)} %get-tuple-element.21), channel_id=1, source_target_pairs={{0,1},{1,2},{2,3},{3,4},{4,5},{5,6},{6,7},{8,9},{9,10},{10,11},{11... | collective-permute-start | bytes 98312 | tf_op jit(solution)/shard_map/ppermute | solution.py:15
  15.0 1.3 %collective-permute-start.1 = (f32[1,4,1,2048]{3,2,1,0:T(1,128)}, f32[1,4,1,2048]{3,2,1,0:T(1,128)}, u32[]{:S(2)}, u32[]{:S(2)}) collective-permute-start(f32[1,4,1,2048]{3,2,1,0:T(1,128)} %get-tuple-element.20), channel_id=1, source_target_pairs={{1,0},{2,1},{3,2},{4,3},{5,4},{6,5},{7,6},{9,8},{10,9},{11,10},{12... | collective-permute-start | bytes 98312 | tf_op jit(solution)/shard_map/ppermute | solution.py:18
  16.4 13.3 %fusion.30 = (f32[1,4,256,2047]{3,2,1,0:T(8,128)}, f32[1,4,256,2047]{3,2,1,0:T(8,128)}) fusion(f32[1,4,256,2048]{3,2,1,0:T(8,128)} %param.8), kind=kLoop, calls=%fused_computation.49 | loop fusion | bytes 33538048 | tf_op jit(solution)/shard_map/jit(_roll_static)/slice | solution.py:29
  29.6 1.4 %fusion.29 = (f32[1,4,256,1]{3,2,1,0:T(8,128)S(1)}, f32[1,4,256,1]{3,2,1,0:T(8,128)S(1)}) fusion(f32[1,4,256,2048]{3,2,1,0:T(8,128)} %param.8), kind=kLoop, calls=%fused_computation.48 | loop fusion | bytes 16384 | tf_op jit(solution)/shard_map/jit(_roll_static)/slice | solution.py:29
  31.8 5.3 %maximum_bitcast_fusion.1 = (f32[256,2048]{1,0:T(8,128)S(1)}, f32[256,2048]{1,0:T(8,128)}, f32[256,2048]{1,0:T(8,128)}, f32[256,2048]{1,0:T(8,128)}) fusion(f32[1,2,256,2048]{3,2,1,0:T(8,128)} %param.9), kind=kLoop, calls=%fused_computation.21 | loop fusion | flops 2097152 | bytes 12582912 | tf_op jit(solution)/shard_map/mul | solution.py:33
  37.8 1.2 collective-permute-start.3
  39.0 2.5 %collective-permute-start.7 = (f32[64,128]{0,1:T(8,128)S(1)}, f32[64,128]{0,1:T(8,128)S(1)}, u32[]{:S(2)}, u32[]{:S(2)}) collective-permute-start(f32[64,128]{0,1:T(8,128)S(1)} %collective-permute-done.6), channel_id=1, source_target_pairs={{0,7},{1,0},{2,1},{3,2},{4,3},{5,4},{6,5},{7,6},{8,15},{9,8},{10,9... | collective-permute-start | bytes 98312 | tf_op jit(solution)/shard_map/ppermute | solution.py:84
  41.5 1.9 %collective-permute-done.3 = f32[64,128]{0,1:T(8,128)S(1)} collective-permute-done((f32[64,128]{0,1:T(8,128)S(1)}, f32[64,128]{0,1:T(8,128)S(1)}, u32[]{:S(2)}, u32[]{:S(2)}) %collective-permute-start.3) | collective-permute-done | bytes 32800 | tf_op jit(solution)/shard_map/ppermute | solution.py:81
  43.4 0.6 fusion.31
  44.0 3.5 %collective-permute-start.8 = (f32[64,128]{0,1:T(8,128)S(1)}, f32[64,128]{0,1:T(8,128)}, u32[]{:S(2)}, u32[]{:S(2)}) collective-permute-start(f32[64,128]{0,1:T(8,128)S(1)} %collective-permute-done.7), channel_id=1, source_target_pairs={{0,7},{1,0},{2,1},{3,2},{4,3},{5,4},{6,5},{7,6},{8,15},{9,8},{10,9... | collective-permute-start | bytes 98312 | tf_op jit(solution)/shard_map/ppermute | solution.py:84
  47.6 1.4 %collective-permute-done.4 = f32[64,128]{0,1:T(8,128)S(1)} collective-permute-done((f32[64,128]{0,1:T(8,128)S(1)}, f32[64,128]{0,1:T(8,128)S(1)}, u32[]{:S(2)}, u32[]{:S(2)}) %collective-permute-start.4) | collective-permute-done | bytes 32800 | tf_op jit(solution)/shard_map/ppermute | solution.py:81
  49.0 2.6 %and_reduce_fusion = pred[]{:T(512)} fusion(s32[4]{0:T(128)} %constant.84.clone.1, s32[1]{0:T(128)} %constant.83.clone.1, s32[1]{0:T(128)} %get-tuple-element.31, s32[1]{0:T(128)} %get-tuple-element.30), kind=kLoop, calls=%fused_computation.37 | loop fusion | flops 27 | bytes 29 | tf_op jit(solution)/shard_map/reduce.1
  51.5 17.9 %psum.14 = f32[64,128]{1,0:T(8,128)} all-reduce(f32[64,128]{1,0:T(8,128)} %broadcast_select_fusion.1), channel_id=1, replica_groups=mesh['zone'=4,'slab'=8] {'zone'}, use_global_device_ids=true, to_apply=%region_1.2 | all-reduce | flops 8192 | bytes 65536 | tf_op jit(solution)/shard_map/psum | solution.py:25
  69.5 2.0 %concatenate.30 = f32[1024,128]{0,1:T(8,128)} concatenate(f32[64,128]{0,1:T(8,128)} %collective-permute-done.5, f32[64,128]{0,1:T(8,128)S(1)} %collective-permute-done.4, f32[64,128]{0,1:T(8,128)S(1)} %collective-permute-done.3, f32[64,128]{0,1:T(8,128)S(1)} %collective-permute-done.2, f32[64,128]{0,1:T(8,128)S(1)} %bitcast.20, f32[64,128]{0,1:T(8,128)S(1)} %collective-permute-done.6, ...), dimensions={0} | concatenate | bytes 1048576 | tf_op jit(solution)/shard_map/jit(_roll_dynamic)/concatenate | solution.py:87
  71.5 0.8 broadcast_in_dim.19
  72.2 1.4 %fusion.14 = f32[128,128]{1,0:T(8,128)S(1)} fusion(f32[128,128]{1,0:T(8,128)S(1)} %bitcast.25, f32[1024,128]{0,1:T(8,128)} %concatenate.30, s32[]{:T(128)S(6)} %select_n.63, s32[128]{0:T(128)S(1)} %fusion.25, pred[128]{0:T(512)(128)(4,1)S(1)} %get-tuple-element.18, f32[128]{0:T(128)S(1)} %get-tuple-element.17), kind=kOutput, calls=%fused_computation.23 | convolution fusion | flops 100827136 | bytes 394372 | tf_op jit(solution)/shard_map/dot_general | solution.py:96
  73.6 1.2 fusion.17
  74.8 21.4 %fusion.6 = f32[1,4,256,2048]{3,2,1,0:T(8,128)} fusion(f32[1,4,256,2048]{3,2,1,0:T(8,128)} %param.8, f32[1,4,1,2048]{3,2,1,0:T(1,128)} %collective-permute-done.1, f32[1,4,1,2048]{3,2,1,0:T(1,128)} %collective-permute-done, f32[1,4,256,1]{3,2,1,0:T(8,128)S(1)} %get-tuple-element.23, f32[1,4,256,2047]{3,2,1,0:T(8,128)} %get-tuple-element.25, ...), kind=kLoop, calls=%fused_computation.7 | loop fusion | flops 48234496 | bytes 42008592 | tf_op jit(solution)/shard_map/sub | solution.py:42
  96.3 14.2 %psum.15 = f32[64,128]{1,0:T(8,128)S(1)} all-reduce(f32[64,128]{1,0:T(8,128)S(1)} %reduce_sum.9), channel_id=1, replica_groups=mesh['zone'=4,'slab'=8] {'zone'}, use_global_device_ids=true, to_apply=%region_4.5 | all-reduce | flops 8192 | bytes 65536 | tf_op jit(solution)/shard_map/psum | solution.py:102
  110.5 0.8 select_subtract_fusion
  111.6 2.2 %broadcast_select_fusion = f32[1,4,1,2048]{3,2,1,0:T(1,128)S(1)} fusion(pred[]{:T(512)} %and_reduce_fusion, f32[1,4,1,2048]{3,2,1,0:T(1,128)S(1)} %reshape.156, f32[1,4,256,2048]{3,2,1,0:T(8,128)} %fusion.6, s32[]{:T(128)} %bitcast.4), kind=kLoop, calls=%fused_computation.32 | loop fusion | flops 16384 | bytes 98309 | tf_op jit(solution)/shard_map/select.1
  113.8 2.4 %scatter-add.4 = f32[1,4,256,2048]{3,2,1,0:T(8,128)} dynamic-update-slice(f32[1,4,256,2048]{3,2,1,0:T(8,128)} %fusion.6, f32[1,4,1,2048]{3,2,1,0:T(1,128)S(1)} %broadcast_select_fusion, s32[]{:T(128)} %constant.81.clone.1, s32[]{:T(128)} %constant.81.clone.1, s32[]{:T(128)} %bitcast.4, s32[]{:T(128)} %constant.81.clone.1) | dynamic-update-slice | bytes 65540 | tf_op jit(solution)/shard_map/scatter-add | solution.py:110
  (38 shorter events, 2.6 us)
Async XLA Ops:
  6.5 104.0 %reduce-scatter.2.cloned.1.call-start = ((), (), s32[]{:S(2)}) async-start(), calls=%async_computation.1 | async-start | bytes 294912 | tf_op jit(solution)/shard_map/reduce_scatter | solution.py:98
  8.5 29.3 %collective-permute-start.2 = (f32[64,128]{0,1:T(8,128)S(1)}, f32[64,128]{0,1:T(8,128)S(1)}, u32[]{:S(2)}, u32[]{:S(2)}) collective-permute-start(f32[64,128]{0,1:T(8,128)S(1)} %bitcast.17), channel_id=1, source_target_pairs={{0,1},{1,2},{2,3},{3,4},{4,5},{5,6},{6,7},{7,0},{8,9},{9,10},{10,1... | collective-permute-start | bytes 98312 | tf_op jit(solution)/shard_map/ppermute | solution.py:81
  9.0 30.0 %collective-permute-start.6 = (f32[64,128]{0,1:T(8,128)S(1)}, f32[64,128]{0,1:T(8,128)S(1)}, u32[]{:S(2)}, u32[]{:S(2)}) collective-permute-start(f32[64,128]{0,1:T(8,128)S(1)} %bitcast.18), channel_id=1, source_target_pairs={{0,7},{1,0},{2,1},{3,2},{4,3},{5,4},{6,5},{7,6},{8,15},{9,8},{10,9... | collective-permute-start | bytes 98312 | tf_op jit(solution)/shard_map/ppermute | solution.py:84
  13.1 61.7 %collective-permute-start = (f32[1,4,1,2048]{3,2,1,0:T(1,128)}, f32[1,4,1,2048]{3,2,1,0:T(1,128)}, u32[]{:S(2)}, u32[]{:S(2)}) collective-permute-start(f32[1,4,1,2048]{3,2,1,0:T(1,128)} %get-tuple-element.21), channel_id=1, source_target_pairs={{0,1},{1,2},{2,3},{3,4},{4,5},{5,6},{6,7},{8,9},{9,10},{10,11},{11... | collective-permute-start | bytes 98312 | tf_op jit(solution)/shard_map/ppermute | solution.py:15
  15.0 59.9 %collective-permute-start.1 = (f32[1,4,1,2048]{3,2,1,0:T(1,128)}, f32[1,4,1,2048]{3,2,1,0:T(1,128)}, u32[]{:S(2)}, u32[]{:S(2)}) collective-permute-start(f32[1,4,1,2048]{3,2,1,0:T(1,128)} %get-tuple-element.20), channel_id=1, source_target_pairs={{1,0},{2,1},{3,2},{4,3},{5,4},{6,5},{7,6},{9,8},{10,9},{11,10},{12... | collective-permute-start | bytes 98312 | tf_op jit(solution)/shard_map/ppermute | solution.py:18
  16.3 14.7 %copy-start = (s32[64,2]{0,1:T(2,128)S(1)}, s32[64,2]{0,1:T(2,128)}, u32[]{:S(2)}) copy-start(s32[64,2]{0,1:T(2,128)} %param.11) | copy-start | bytes 1540
  16.3 15.0 %copy-start.1 = (f32[64,2]{0,1:T(2,128)S(1)}, f32[64,2]{0,1:T(2,128)}, u32[]{:S(2)}) copy-start(f32[64,2]{0,1:T(2,128)} %param.13) | copy-start | bytes 1540
  16.3 15.2 %copy-start.2 = (s32[64,2]{0,1:T(2,128)S(1)}, s32[64,2]{0,1:T(2,128)}, u32[]{:S(2)}) copy-start(s32[64,2]{0,1:T(2,128)} %param.12) | copy-start | bytes 1540
  29.6 45.2 %copy-start.3 = (f32[4]{0:T(128)S(1)}, f32[4]{0:T(128)}, u32[]{:S(2)}) copy-start(f32[4]{0:T(128)} %param.10) | copy-start | bytes 52
  37.8 5.6 %collective-permute-start.3 = (f32[64,128]{0,1:T(8,128)S(1)}, f32[64,128]{0,1:T(8,128)S(1)}, u32[]{:S(2)}, u32[]{:S(2)}) collective-permute-start(f32[64,128]{0,1:T(8,128)S(1)} %collective-permute-done.2), channel_id=1, source_target_pairs={{0,1},{1,2},{2,3},{3,4},{4,5},{5,6},{6,7},{7,0},{8,9},{9,10},{10,1... | collective-permute-start | bytes 98312 | tf_op jit(solution)/shard_map/ppermute | solution.py:81
  39.0 5.1 %collective-permute-start.7 = (f32[64,128]{0,1:T(8,128)S(1)}, f32[64,128]{0,1:T(8,128)S(1)}, u32[]{:S(2)}, u32[]{:S(2)}) collective-permute-start(f32[64,128]{0,1:T(8,128)S(1)} %collective-permute-done.6), channel_id=1, source_target_pairs={{0,7},{1,0},{2,1},{3,2},{4,3},{5,4},{6,5},{7,6},{8,15},{9,8},{10,9... | collective-permute-start | bytes 98312 | tf_op jit(solution)/shard_map/ppermute | solution.py:84
  43.4 5.6 %collective-permute-start.4 = (f32[64,128]{0,1:T(8,128)S(1)}, f32[64,128]{0,1:T(8,128)S(1)}, u32[]{:S(2)}, u32[]{:S(2)}) collective-permute-start(f32[64,128]{0,1:T(8,128)S(1)} %collective-permute-done.3), channel_id=1, source_target_pairs={{0,1},{1,2},{2,3},{3,4},{4,5},{5,6},{6,7},{7,0},{8,9},{9,10},{10,1... | collective-permute-start | bytes 98312 | tf_op jit(solution)/shard_map/ppermute | solution.py:81
  44.0 25.4 %collective-permute-start.8 = (f32[64,128]{0,1:T(8,128)S(1)}, f32[64,128]{0,1:T(8,128)}, u32[]{:S(2)}, u32[]{:S(2)}) collective-permute-start(f32[64,128]{0,1:T(8,128)S(1)} %collective-permute-done.7), channel_id=1, source_target_pairs={{0,7},{1,0},{2,1},{3,2},{4,3},{5,4},{6,5},{7,6},{8,15},{9,8},{10,9... | collective-permute-start | bytes 98312 | tf_op jit(solution)/shard_map/ppermute | solution.py:84
  49.0 20.5 %collective-permute-start.5 = (f32[64,128]{0,1:T(8,128)S(1)}, f32[64,128]{0,1:T(8,128)}, u32[]{:S(2)}, u32[]{:S(2)}) collective-permute-start(f32[64,128]{0,1:T(8,128)S(1)} %collective-permute-done.4), channel_id=1, source_target_pairs={{0,1},{1,2},{2,3},{3,4},{4,5},{5,6},{6,7},{7,0},{8,9},{9,10},{10,1... | collective-permute-start | bytes 98312 | tf_op jit(solution)/shard_map/ppermute | solution.py:81
Sparse Core Ops, SparseCore 0:
  74.9 26.6 reduce-scatter.1
